TPU v7x, 32 devices: a whole 2x2x4 slice. The times are simulated.
32 devices in a mesh: row: 4 (over z), col: 8 (over y, x, core).
Axes of the slice: x: 2, y: 2, z: 4, core: 2. Of those that a mesh axis runs over, the one named last changes fastest.
Arguments:
- occupations: int32 [4096, 128], P('row'), may hold values from 0 to 2
- table: float32 [384, 1024], replicated, may hold values from -0.5 to 0.5
- weights: float32 [2, 1024, 4096], P(None, None, 'col'), may hold values from -0.1875 to 0.1875
- biases: float32 [2, 4096], P(None, 'col'), may hold values from -6 to 6
- heads: float32 [2, 4096], P(None, 'col'), may hold values from -18 to 18
- energies: float32 [4096], P('row'), may hold values from -6 to 6
Outputs:
- schur: float32 [4096, 4096], P('row', 'col')
- solved_rhs: float32 [4096], P('row')
All inputs are finite; a program needn't handle non-finite values.
Results may differ from a plain program's by a relative error of at most 0.0034.
Values may be sent and summed in bfloat16 or wider, within the bound.
A program may use at most 128 MiB of HBM per device.

v0:
```python
import math
import jax
import jax.numpy as jnp
from jax import lax
from jax.sharding import PartitionSpec as P

norm_eps = 1e-06
diag_shift = 0.05


def broadcast(block, axis, holder):
    block = jnp.where(lax.axis_index(axis) == holder, block, jnp.zeros_like(block))
    return lax.psum(block, axis)


def jacobian(occupations, table, weights, biases, heads):
    onehot = jnp.concatenate(
        [
            (occupations == 0).astype(jnp.float32),
            (occupations == 1).astype(jnp.float32),
            (occupations == 2).astype(jnp.float32),
        ],
        axis=1,
    )
    embedded = jnp.dot(
        onehot, table, precision=lax.Precision.HIGHEST, preferred_element_type=jnp.float32
    )
    embedded = embedded * lax.rsqrt(
        jnp.mean(embedded * embedded, axis=-1, keepdims=True) + norm_eps
    )
    blocks = []
    for panel_index in range(2):
        hidden = (
            jnp.dot(
                embedded,
                weights[panel_index],
                precision=lax.Precision.HIGHEST,
                preferred_element_type=jnp.float32,
            )
            + biases[panel_index]
        )
        blocks.append(heads[panel_index] * jax.nn.sigmoid(hidden))
    return jnp.concatenate(blocks, axis=1)


def on_device(occupations, table, weights, biases, heads, energies):
    row_count = occupations.shape[0]
    row_devices = lax.axis_size("row")
    col_devices = lax.axis_size("col")
    sample_total = row_count * row_devices
    panel_width = sample_total // col_devices
    derivs = jacobian(occupations, table, weights, biases, heads)
    col_sums = lax.psum(jnp.sum(derivs, axis=0), "row")
    centered = ((derivs - col_sums / sample_total) * (1.0 / math.sqrt(sample_total))).astype(
        jnp.bfloat16
    )
    own_rows = lax.all_gather(centered, "col", axis=1, tiled=True)
    every_sample = lax.all_gather(centered, "row", axis=0, tiled=True)
    partner = lax.all_to_all(every_sample, "col", split_axis=0, concat_axis=1, tiled=True)
    kernel = lax.dot_general(
        own_rows, partner, (((1,), (1,)), ((), ())), preferred_element_type=jnp.float32
    )
    row_ids = lax.axis_index("row") * row_count + lax.iota(jnp.int32, row_count)
    col_ids = lax.axis_index("col") * panel_width + lax.iota(jnp.int32, panel_width)
    kernel = kernel + jnp.where(row_ids[:, None] == col_ids[None, :], diag_shift, 0.0).astype(
        jnp.float32
    )
    right_side = energies
    for panel_index in range(2):
        start_global = panel_index * panel_width
        root_row = start_global // row_count
        offset = start_global % row_count
        top_block, top_side = (
            broadcast(kernel[offset : offset + panel_width], "row", root_row),
            broadcast(right_side[offset : offset + panel_width], "row", root_row),
        )
        column, diag_block = (
            broadcast(kernel, "col", panel_index),
            broadcast(top_block, "col", panel_index),
        )
        factor = jnp.linalg.cholesky(diag_block)
        left_rows = lax.linalg.triangular_solve(
            factor, column, left_side=False, lower=True, transpose_a=True
        )
        right_rows = lax.linalg.triangular_solve(
            factor, top_block.T, left_side=False, lower=True, transpose_a=True
        )
        kernel = kernel - lax.dot_general(
            left_rows,
            right_rows,
            (((1,), (1,)), ((), ())),
            precision=lax.Precision.HIGHEST,
            preferred_element_type=jnp.float32,
        )
        solved = lax.linalg.triangular_solve(factor, top_side[:, None], left_side=True, lower=True)[
            :, 0
        ]
        right_side = right_side - jnp.dot(
            left_rows, solved, precision=lax.Precision.HIGHEST, preferred_element_type=jnp.float32
        )
        placed = right_side.at[offset : offset + panel_width].set(solved)
        right_side = jnp.where(lax.axis_index("row") == root_row, placed, right_side)
    return (kernel, right_side)


def solution(mesh):
    placed = (P("row", None), P(), P(None, None, "col"), P(None, "col"), P(None, "col"), P("row"))
    return jax.shard_map(
        on_device,
        mesh=mesh,
        in_specs=placed,
        out_specs=(P("row", "col"), P("row")),
        check_vma=False,
    )
```

profile of v0, /device:TPU:0, one launch (start us, length us, event | category | flops | bytes accessed | tf_op | source)
XLA Modules:
  0.0 969.1 jit_solution(3831402307478594253)
XLA Ops:
  8.7 5.1 multiply_reduce_fusion
  13.9 12.5 %divide_multiply_fusion.1 = f32[1024,512]{0,1:T(8,128)S(1)} fusion(f32[2,1024,512]{2,1,0:T(8,128)} %param.19, f32[1024,1024]{0,1:T(8,128)} %get-tuple-element.136, f32[1024]{0:T(1024)S(1)} %add_rsqrt_fusion, f32[512]{0:T(512)S(1)} %bitcast.291, f32[512]{0:T(512)S(1)} %bitcast.290), kind=kOutput, calls=%fused_computation.20 | convolution fusion | flops 6446120960 | bytes 8396800 | tf_op jit(solution)/shard_map/dot_general | solution.py:34
  26.4 7.2 divide_multiply_fusion
  35.6 13.7 %all-reduce.3 = (f32[1024]{0:T(1024)S(1)}, f32[512,1]{0,1:T(1,128)S(1)}) all-reduce(f32[1024]{0:T(1024)S(1)} %fusion.4, f32[512,1]{0,1:T(1,128)S(1)} %bitcast.282), channel_id=1, replica_groups=mesh['row'=4,'col'=8] {'row'}, use_global_device_ids=true, to_apply=%region_2.0 | all-reduce | flops 1536 | bytes 12288 | tf_op jit(solution)/shard_map/psum | solution.py:53
  49.4 3.9 multiply_convert_fusion
  54.1 147.2 %all-gather.5.cloned.1.call-done = bf16[4096,1024]{0,1:T(8,128)(2,1)} async-done(((bf16[1024,1024]{0,1:T(8,128)(2,1)}), bf16[4096,1024]{0,1:T(8,128)(2,1)}) %all-gather.5.cloned.1.call-update) | async-done | bytes 8388624 | tf_op jit(solution)/shard_map/all_gather | solution.py:58
  201.3 7.9 copy.26
  209.1 5.0 all-to-all-start
  214.2 126.8 %all-to-all-done = bf16[8,512,1024]{1,2,0:T(8,128)(2,1)} async-done(((bf16[8,512,1024]{1,2,0:T(8,128)(2,1)}), bf16[8,512,1024]{1,2,0:T(8,128)(2,1)}, u32[]{:S(2)}, u32[]{:S(2)}) %all-to-all-start) | async-done | bytes 8388640 | tf_op jit(solution)/shard_map/all_to_all | solution.py:59
  341.0 32.8 %all-gather.3.cloned.1.call-done = bf16[1024,8192]{0,1:T(8,128)(2,1)} async-done(((bf16[1024,1024]{0,1:T(8,128)(2,1)}), bf16[1024,8192]{0,1:T(8,128)(2,1)}) %all-gather.3.cloned.1.call-update) | async-done | bytes 16777232 | tf_op jit(solution)/shard_map/all_gather | solution.py:57
  373.8 15.9 %broadcast_select_fusion.1 = (f32[1024,512]{0,1:T(8,128)}, f32[1024,512]{0,1:T(8,128)S(1)}) fusion(pred[]{:T(512)S(6)} %eq.56, s32[512]{0:T(512)S(1)} %iota_add_fusion.1, s32[1024]{0:T(1024)S(1)} %iota_add_fusion, bf16[1024,8192]{0,1:T(8,128)(2,1)} %all-gather.3.cloned.1.call-done, bf16[512,8192]{0,1:T(8,128)(2,1)} %bitcast.7), kind=kOutput, calls=%fused_computation.118 | convolution fusion | flops 8592031744 | bytes 29366272 | tf_op jit(solution)/shard_map/dot_general | solution.py:60
  392.2 51.6 %all-reduce.9.cloned.1.call-done = f32[512,512]{0,1:T(8,128)} async-done(((f32[512,512]{0,1:T(8,128)}), f32[512,512]{0,1:T(8,128)}) %all-reduce.9.cloned.1.call-update) | async-done | bytes 1048592 | tf_op jit(solution)/shard_map/psum | solution.py:13
  443.8 2.3 broadcast_select_fusion.3
  446.6 69.6 %all-reduce.15.cloned.1.call-done = (f32[1024,512]{0,1:T(8,128)}, f32[512,512]{0,1:T(8,128)}) async-done(((f32[1024,512]{0,1:T(8,128)}, f32[512,512]{0,1:T(8,128)}), (f32[1024,512]{0,1:T(8,128)}, f32[512,512]{0,1:T(8,128)})) %all-reduce.15.cloned.1.call-update) | async-done | bytes 3145744 | tf_op jit(solution)/shard_map/psum | solution.py:13
  516.2 1.6 copy.16
  519.1 11.7 %cholesky.286 = f32[128,128]{1,0:T(8,128)S(1)} custom-call(f32[128,128]{1,0:T(8,128)S(1)} %cholesky.426), custom_call_target="Cholesky" | custom-call | tf_op jit(solution)/shard_map/jit(cholesky)/cholesky | solution.py:81
  531.0 9.8 %custom-call.35 = f32[1,128,128]{1,2,0:T(8,128)S(1)} custom-call(f32[1,128,128]{2,1,0:T(8,128)S(1)} %get-tuple-element.130), custom_call_target="InvertDiagBlocksLowerTriangular" | custom-call | tf_op jit(solution)/shard_map/jit(cholesky)/cholesky | solution.py:81
  543.3 11.7 %cholesky.305 = f32[128,128]{1,0:T(8,128)S(1)} custom-call(f32[128,128]{1,0:T(8,128)S(1)} %cholesky.430), custom_call_target="Cholesky" | custom-call | tf_op jit(solution)/shard_map/jit(cholesky)/cholesky | solution.py:81
  555.1 10.0 %custom-call.36 = f32[1,128,128]{1,2,0:T(8,128)S(1)} custom-call(f32[1,128,128]{2,1,0:T(8,128)S(1)} %get-tuple-element.127), custom_call_target="InvertDiagBlocksLowerTriangular" | custom-call | tf_op jit(solution)/shard_map/jit(cholesky)/cholesky | solution.py:81
  566.6 11.7 %cholesky.326 = f32[128,128]{1,0:T(8,128)S(1)} custom-call(f32[128,128]{1,0:T(8,128)S(1)} %cholesky.435), custom_call_target="Cholesky" | custom-call | tf_op jit(solution)/shard_map/jit(cholesky)/cholesky | solution.py:81
  579.0 9.8 %custom-call.37 = f32[1,128,128]{1,2,0:T(8,128)S(1)} custom-call(f32[1,128,128]{2,1,0:T(8,128)S(1)} %get-tuple-element.124), custom_call_target="InvertDiagBlocksLowerTriangular" | custom-call | tf_op jit(solution)/shard_map/jit(cholesky)/cholesky | solution.py:81
  590.3 11.7 %cholesky.343 = f32[128,128]{1,0:T(8,128)S(1)} custom-call(f32[128,128]{1,0:T(8,128)S(1)} %convolution_subtract_fusion.17), custom_call_target="Cholesky" | custom-call | tf_op jit(solution)/shard_map/jit(cholesky)/cholesky | solution.py:81
  606.6 8.0 while.14
  614.7 39.3 %custom-call.38 = f32[4,128,128]{1,2,0:T(8,128)S(1)} custom-call(f32[4,128,128]{2,1,0:T(8,128)S(1)} %get-tuple-element.72), custom_call_target="InvertDiagBlocksLowerTriangular" | custom-call | tf_op jit(solution)/shard_map/triangular_solve/custom-call.3 | solution.py:82
  654.0 1.7 fusion.85
  655.7 1.6 convolution_subtract_fusion.5
  657.9 1.8 convolution_subtract_fusion.3
  660.3 2.3 fusion.32
  666.2 1.5 convolution_subtract_fusion.11
  668.1 5.1 broadcast_select_fusion
  676.3 51.5 %all-reduce.11.cloned.1.call-done = f32[512,512]{0,1:T(8,128)} async-done(((f32[512,512]{0,1:T(8,128)}), f32[512,512]{0,1:T(8,128)}) %all-reduce.11.cloned.1.call-update) | async-done | bytes 1048592 | tf_op jit(solution)/shard_map/psum | solution.py:13
  731.1 10.1 %psum.71 = f32[512,1]{0,1:T(1,128)S(1)} all-reduce(f32[512,1]{0,1:T(1,128)S(1)} %bitcast.285), channel_id=1, replica_groups=mesh['row'=4,'col'=8] {'row'}, use_global_device_ids=true, to_apply=%region_18.23 | all-reduce | flops 512 | bytes 4096 | tf_op jit(solution)/shard_map/psum | solution.py:13
  741.3 58.9 %all-reduce.13.cloned.1.call-done = (f32[1024,512]{0,1:T(8,128)}, f32[512,512]{0,1:T(8,128)}) async-done(((f32[1024,512]{0,1:T(8,128)}, f32[512,512]{0,1:T(8,128)}), (f32[1024,512]{0,1:T(8,128)}, f32[512,512]{0,1:T(8,128)})) %all-reduce.13.cloned.1.call-update) | async-done | bytes 3145744 | tf_op jit(solution)/shard_map/psum | solution.py:13
  800.2 1.6 copy.18
  803.1 11.7 %cholesky.358 = f32[128,128]{1,0:T(8,128)S(1)} custom-call(f32[128,128]{1,0:T(8,128)S(1)} %cholesky.439), custom_call_target="Cholesky" | custom-call | tf_op jit(solution)/shard_map/jit(cholesky)/cholesky | solution.py:81
  815.0 9.8 %custom-call.40 = f32[1,128,128]{1,2,0:T(8,128)S(1)} custom-call(f32[1,128,128]{2,1,0:T(8,128)S(1)} %get-tuple-element.120), custom_call_target="InvertDiagBlocksLowerTriangular" | custom-call | tf_op jit(solution)/shard_map/jit(cholesky)/cholesky | solution.py:81
  827.3 11.7 %cholesky.377 = f32[128,128]{1,0:T(8,128)S(1)} custom-call(f32[128,128]{1,0:T(8,128)S(1)} %cholesky.443), custom_call_target="Cholesky" | custom-call | tf_op jit(solution)/shard_map/jit(cholesky)/cholesky | solution.py:81
  840.4 10.2 %custom-call.41 = f32[1,128,128]{1,2,0:T(8,128)S(1)} custom-call(f32[1,128,128]{2,1,0:T(8,128)S(1)} %get-tuple-element.117), custom_call_target="InvertDiagBlocksLowerTriangular" | custom-call | tf_op jit(solution)/shard_map/jit(cholesky)/cholesky | solution.py:81
  852.2 11.7 %cholesky.398 = f32[128,128]{1,0:T(8,128)S(1)} custom-call(f32[128,128]{1,0:T(8,128)S(1)} %cholesky.448), custom_call_target="Cholesky" | custom-call | tf_op jit(solution)/shard_map/jit(cholesky)/cholesky | solution.py:81
  864.7 9.8 %custom-call.42 = f32[1,128,128]{1,2,0:T(8,128)S(1)} custom-call(f32[1,128,128]{2,1,0:T(8,128)S(1)} %get-tuple-element.114), custom_call_target="InvertDiagBlocksLowerTriangular" | custom-call | tf_op jit(solution)/shard_map/jit(cholesky)/cholesky | solution.py:81
  875.9 11.7 %cholesky.415 = f32[128,128]{1,0:T(8,128)S(1)} custom-call(f32[128,128]{1,0:T(8,128)S(1)} %convolution_subtract_fusion.16), custom_call_target="Cholesky" | custom-call | tf_op jit(solution)/shard_map/jit(cholesky)/cholesky | solution.py:81
  891.3 8.0 while.15
  899.3 39.3 %custom-call.43 = f32[4,128,128]{1,2,0:T(8,128)S(1)} custom-call(f32[4,128,128]{2,1,0:T(8,128)S(1)} %get-tuple-element.74), custom_call_target="InvertDiagBlocksLowerTriangular" | custom-call | tf_op jit(solution)/shard_map/triangular_solve/custom-call.3 | solution.py:82
  940.1 1.7 fusion.83
  941.8 1.6 convolution_subtract_fusion.4
  951.3 1.5 convolution_subtract_fusion.10
  953.3 5.2 convolution_subtract_fusion
  958.5 2.9 copy.20
  (180 shorter events, 64.6 us)
Async XLA Ops:
  7.2 1.6 copy-start
  7.2 194.1 %all-gather.5.cloned.1.call-start = ((), (), s32[]{:S(2)}) async-start(), calls=%async_computation.2 | async-start | bytes 10485760 | tf_op jit(solution)/shard_map/all_gather | solution.py:58
  8.7 5.1 copy-start.19
  8.7 5.1 copy-start.20
  13.8 12.6 %copy-start.21 = (f32[2,1024,512]{2,1,0:T(8,128)S(1)}, f32[2,1024,512]{2,1,0:T(8,128)}, u32[]{:S(2)}) copy-start(f32[2,1024,512]{2,1,0:T(8,128)} %param.19) | copy-start | bytes 12582916
  13.9 12.6 %copy-start.22 = (f32[1024,1024]{0,1:T(8,128)S(1)}, f32[1024,1024]{0,1:T(8,128)}, u32[]{:S(2)}) copy-start(f32[1024,1024]{0,1:T(8,128)} %get-tuple-element.136) | copy-start | bytes 12582916
  26.4 7.2 copy-start.4
  33.6 1.3 copy-start.5
  34.9 0.7 copy-start.17
  53.3 320.5 %all-gather.3.cloned.1.call-start = ((), (), s32[]{:S(2)}) async-start(), calls=%async_computation.1 | async-start | bytes 18874368 | tf_op jit(solution)/shard_map/all_gather | solution.py:57
  209.1 131.9 %all-to-all-start = ((bf16[8,512,1024]{1,2,0:T(8,128)(2,1)}), bf16[8,512,1024]{1,2,0:T(8,128)(2,1)}, u32[]{:S(2)}, u32[]{:S(2)}) async-start(bf16[8,512,1024]{1,2,0:T(8,128)(2,1)} %bitcast.258), calls=%async_computation | async-start | bytes 16777216 | tf_op jit(solution)/shard_map/all_to_all | solution.py:59
  214.1 229.6 %all-reduce.9.cloned.1.call-start = ((), (), s32[]{:S(2)}) async-start(), calls=%async_computation.3 | async-start | bytes 2097152 | tf_op jit(solution)/shard_map/psum | solution.py:13
  389.7 1.4 copy-start.6
  392.2 124.1 %all-reduce.15.cloned.1.call-start = ((), (), s32[]{:S(2)}) async-start(), calls=%async_computation.6 | async-start | bytes 6291456 | tf_op jit(solution)/shard_map/psum | solution.py:13
  446.1 281.7 %all-reduce.11.cloned.1.call-start = ((), (), s32[]{:S(2)}) async-start(), calls=%async_computation.4 | async-start | bytes 2097152 | tf_op jit(solution)/shard_map/psum | solution.py:13
  516.2 1.7 copy-start.9
  518.1 1.0 copy-start.13
  660.3 2.9 copy-start.11
  663.3 4.8 copy-start.14
  664.3 3.7 copy-start.7
  673.2 1.4 copy-start.2
  675.7 124.5 %all-reduce.13.cloned.1.call-start = ((), (), s32[]{:S(2)}) async-start(), calls=%async_computation.5 | async-start | bytes 6291456 | tf_op jit(solution)/shard_map/psum | solution.py:13
  728.9 1.0 copy-start.15
  800.2 1.7 copy-start.8
  802.1 1.0 copy-start.12
  939.4 4.7 copy-start.16
  946.6 1.8 copy-start.10
  949.5 3.8 copy-start.3
  953.3 8.7 copy-start.1
  961.4 0.6 copy-start.18
Sparse Core Ops, SparseCore 0:
  53.5 147.7 all-gather.4
  203.1 170.6 all-gather.2
  392.3 51.4 all-reduce.8
  447.6 68.6 all-reduce.14
  675.8 51.9 all-reduce.10
  731.6 68.6 all-reduce.12
where the time goes:
time: 975 us; the launch traced here: 969 us
  waiting for transfers between devices  539 us (55%)
  other arithmetic  249 us (26%)
  matrix products  92.9 us (10%)
  local copies, waits for them, and re-layouts  37.6 us (4%)
  blocking collectives  23.8 us (2%)
  between operations  20.4 us (2%)
    psum x4, waiting for transfers between devices, broadcast(): return lax.psum(block, axis)  232 us
    another operation x29, other arithmetic, on_device(): factor = jnp.linalg.cholesky(diag_block)  158 us
    all_gather x1, waiting for transfers between devices, on_device(): every_sample = lax.all_gather(centered, 'row', axis=0, tiled=True)  147 us
    all_to_all x1, waiting for transfers between devices, on_device(): lax.all_to_all(every_sample, 'col', split_axis=0, concat_axis=1, tiled=True)  127 us
    another operation x5, other arithmetic, on_device(): lax.linalg.triangular_solve(factor, column, left_side=False, lower=True,...  79.4 us
    all_gather x1, waiting for transfers between devices, on_device(): own_rows = lax.all_gather(centered, 'col', axis=1, tiled=True)  32.8 us
    dot_general x2, matrix products, jacobian(): jnp.dot(embedded, weights[panel_index], precision=lax.Precision.HIGHEST,...  19.7 us
  transfers between devices with their start and end apart: 7, of which 7 were waited for; matrix products, arithmetic and copies ran while one was open for 1% of the time, Pallas kernels for 0%

commit v1 on v0

--- a/solution.py
+++ b/solution.py
@@ -10,7 +10,10 @@
 
 def broadcast(block, axis, holder):
     block = jnp.where(lax.axis_index(axis) == holder, block, jnp.zeros_like(block))
-    return lax.psum(block, axis)
+    part_the_task = lambda vector, axis_tag: jnp.sum(
+        lax.all_gather(vector, axis_name=axis_tag), axis=0
+    )
+    return part_the_task(block, axis)
 
 
 def jacobian(occupations, table, weights, biases, heads):

time: 975 us -> 1040 us (1.067)
  other arithmetic: 249 us -> 285 us
  blocking collectives: 23.8 us -> 37.8 us
    all_gather x0 -> x6, waiting for transfers between devices: none -> 237 us  [broadcast(): lax.all_gather(vector, axis_name=axis_tag)]
    psum x4 -> x0, waiting for transfers between devices: 232 us -> none  [broadcast(): return lax.psum(block, axis)]
    reduce_sum x0 -> x8, other arithmetic: none -> 33.4 us  [broadcast(): jnp.sum(lax.all_gather(vector, axis_name=axis_tag), axis=0)]
    all_gather x0 -> x2, blocking collectives: none -> 24.3 us  [broadcast(): lax.all_gather(vector, axis_name=axis_tag)]
  transfers between devices with their start and end apart: 7 -> 9, of which waited for: 7 -> 7; matrix products, arithmetic and copies ran while one was open for 1% -> 30% of each run, Pallas kernels for 0% -> 0%
where the time goes in v1:
time: 1040 us; the launch traced here: 1030 us
  waiting for transfers between devices  546 us (52%)
  other arithmetic  285 us (27%)
  matrix products  95.1 us (9%)
  local copies, waits for them, and re-layouts  40.8 us (4%)
  blocking collectives  37.8 us (4%)
  between operations  20.2 us (2%)
    all_gather x6, waiting for transfers between devices, broadcast(): lax.all_gather(vector, axis_name=axis_tag)  237 us
    another operation x29, other arithmetic, on_device(): factor = jnp.linalg.cholesky(diag_block)  158 us
    all_gather x1, waiting for transfers between devices, on_device(): every_sample = lax.all_gather(centered, 'row', axis=0, tiled=True)  147 us
    all_to_all x1, waiting for transfers between devices, on_device(): lax.all_to_all(every_sample, 'col', split_axis=0, concat_axis=1, tiled=True)  127 us
    another operation x5, other arithmetic, on_device(): lax.linalg.triangular_solve(factor, column, left_side=False, lower=True,...  80.9 us
    reduce_sum x8, other arithmetic, broadcast(): jnp.sum(lax.all_gather(vector, axis_name=axis_tag), axis=0)  33.4 us
    all_gather x1, waiting for transfers between devices, on_device(): own_rows = lax.all_gather(centered, 'col', axis=1, tiled=True)  32.8 us
    all_gather x2, blocking collectives, broadcast(): lax.all_gather(vector, axis_name=axis_tag)  24.3 us
  transfers between devices with their start and end apart: 9, of which 7 were waited for; matrix products, arithmetic and copies ran while one was open for 30% of the time, Pallas kernels for 0%

profile of v1, /device:TPU:0, one launch (start us, length us, event | category | flops | bytes accessed | tf_op | source)
XLA Modules:
  0.0 1030.9 jit_solution(442244637369376050)
XLA Ops:
  8.7 3.5 multiply_reduce_fusion
  12.3 7.2 divide_multiply_fusion.1
  19.5 7.5 divide_multiply_fusion
  28.7 13.5 %psum.7 = f32[1024]{0:T(1024)S(1)} all-reduce(f32[1024]{0:T(1024)S(1)} %fusion.4), channel_id=1, replica_groups=mesh['row'=4,'col'=8] {'row'}, use_global_device_ids=true, to_apply=%region_2.0 | all-reduce | flops 1024 | bytes 8192 | tf_op jit(solution)/shard_map/psum | solution.py:56
  42.1 3.9 multiply_convert_fusion
  46.9 147.2 %all-gather.21.cloned.1.call-done = bf16[4096,1024]{0,1:T(8,128)(2,1)} async-done(((bf16[1024,1024]{0,1:T(8,128)(2,1)}), bf16[4096,1024]{0,1:T(8,128)(2,1)}) %all-gather.21.cloned.1.call-update) | async-done | bytes 8388624 | tf_op jit(solution)/shard_map/all_gather | solution.py:61
  194.1 7.9 copy.30
  202.0 5.0 all-to-all-start
  207.1 126.8 %all-to-all-done = bf16[8,512,1024]{1,2,0:T(8,128)(2,1)} async-done(((bf16[8,512,1024]{1,2,0:T(8,128)(2,1)}), bf16[8,512,1024]{1,2,0:T(8,128)(2,1)}, u32[]{:S(2)}, u32[]{:S(2)}) %all-to-all-start) | async-done | bytes 8388640 | tf_op jit(solution)/shard_map/all_to_all | solution.py:62
  333.8 32.8 %all-gather.19.cloned.1.call-done = bf16[1024,8192]{0,1:T(8,128)(2,1)} async-done(((bf16[1024,1024]{0,1:T(8,128)(2,1)}), bf16[1024,8192]{0,1:T(8,128)(2,1)}) %all-gather.19.cloned.1.call-update) | async-done | bytes 16777232 | tf_op jit(solution)/shard_map/all_gather | solution.py:60
  366.7 15.9 %broadcast_select_fusion.1 = (f32[1024,512]{1,0:T(8,128)}, f32[1024,512]{1,0:T(8,128)S(1)}) fusion(pred[]{:T(512)S(6)} %eq.56, s32[512]{0:T(512)S(1)} %iota_add_fusion.1, s32[1024]{0:T(1024)S(1)} %iota_add_fusion, bf16[1024,8192]{0,1:T(8,128)(2,1)} %all-gather.19.cloned.1.call-done, bf16[512,8192]{0,1:T(8,128)(2,1)} %bitcast.7), kind=kOutput, calls=%fused_computation.118 | convolution fusion | flops 8592031744 | bytes 29366272 | tf_op jit(solution)/shard_map/dot_general | solution.py:63
  385.1 80.4 %all-gather.23.cloned.1.call-done = f32[2048,512]{1,0:T(8,128)} async-done(((f32[512,512]{1,0:T(8,128)}), f32[2048,512]{1,0:T(8,128)}) %all-gather.23.cloned.1.call-update) | async-done | bytes 4194320 | tf_op jit(solution)/shard_map/all_gather | solution.py:14
  465.5 2.8 reduce_sum.92
  470.2 52.1 %all-gather.25.cloned.1.call-done = f32[4096,512]{1,0:T(8,128)} async-done(((f32[512,512]{1,0:T(8,128)}), f32[4096,512]{1,0:T(8,128)}) %all-gather.25.cloned.1.call-update) | async-done | bytes 8388624 | tf_op jit(solution)/shard_map/all_gather | solution.py:14
  522.3 4.5 reduce_sum.93
  530.5 11.7 %cholesky.286 = f32[128,128]{1,0:T(8,128)S(1)} custom-call(f32[128,128]{1,0:T(8,128)S(1)} %cholesky.426), custom_call_target="Cholesky" | custom-call | tf_op jit(solution)/shard_map/jit(cholesky)/cholesky | solution.py:84
  542.4 9.8 custom-call.35
  554.8 12.1 %cholesky.305 = f32[128,128]{1,0:T(8,128)S(1)} custom-call(f32[128,128]{1,0:T(8,128)S(1)} %cholesky.430), custom_call_target="Cholesky" | custom-call | tf_op jit(solution)/shard_map/jit(cholesky)/cholesky | solution.py:84
  566.9 9.8 custom-call.36
  578.3 11.7 %cholesky.326 = f32[128,128]{1,0:T(8,128)S(1)} custom-call(f32[128,128]{1,0:T(8,128)S(1)} %cholesky.435), custom_call_target="Cholesky" | custom-call | tf_op jit(solution)/shard_map/jit(cholesky)/cholesky | solution.py:84
  590.0 9.8 custom-call.37
  601.3 11.9 %cholesky.343 = f32[128,128]{1,0:T(8,128)S(1)} custom-call(f32[128,128]{1,0:T(8,128)S(1)} %convolution_subtract_fusion.17), custom_call_target="Cholesky" | custom-call | tf_op jit(solution)/shard_map/jit(cholesky)/cholesky | solution.py:84
  618.6 11.5 %while.14 = (s32[]{:T(128)}, f32[512,512]{1,0:T(8,128)}, s32[4,2]{0,1:T(2,128)S(1)}, f32[4,128,128]{2,1,0:T(8,128)S(1)}, s32[]{:T(128)}) while((s32[]{:T(128)}, f32[512,512]{1,0:T(8,128)}, s32[4,2]{0,1:T(2,128)S(1)}, f32[4,128,128]{2,1,0:T(8,128)S(1)}, s32[]{:T(128)}) %tuple.86), condition=%wide.while_cond.2, body=%wide.while_body.2.sunk | while | flops 2 | bytes 131181 | solution.py:85
  630.1 39.3 %custom-call.38 = f32[4,128,128]{1,2,0:T(8,128)S(1)} custom-call(f32[4,128,128]{2,1,0:T(8,128)S(1)} %get-tuple-element.72), custom_call_target="InvertDiagBlocksLowerTriangular" | custom-call | tf_op jit(solution)/shard_map/triangular_solve/custom-call.3 | solution.py:85
  674.2 9.4 reduce_sum.94
  691.5 2.9 fusion.32
  695.1 4.8 broadcast_select_fusion
  702.5 80.9 %all-gather.29.cloned.1.call-done = f32[2048,512]{1,0:T(8,128)} async-done(((f32[512,512]{1,0:T(8,128)}), f32[2048,512]{1,0:T(8,128)}) %all-gather.29.cloned.1.call-update) | async-done | bytes 4194320 | tf_op jit(solution)/shard_map/all_gather | solution.py:14
  783.3 2.8 reduce_sum.95
  788.0 11.9 %all-gather.8 = f32[4,1,512]{2,1,0:T(1,128)S(1)} all-gather(f32[1,1,512]{2,1,0:T(1,128)S(1)} %bitcast.304), channel_id=8, replica_groups=mesh['row'=4,'col'=8] {'row'}, dimensions={0}, use_global_device_ids=true | all-gather | bytes 10240 | tf_op jit(solution)/shard_map/all_gather | solution.py:14
  801.4 2.4 fusion.36
  803.8 12.3 %all-gather.9 = f32[4,1,512]{2,1,0:T(1,128)S(1)} all-gather(f32[1,1,512]{2,1,0:T(1,128)S(1)} %bitcast.305), channel_id=9, replica_groups=mesh['row'=4,'col'=8] {'row'}, dimensions={0}, use_global_device_ids=true | all-gather | bytes 10240 | tf_op jit(solution)/shard_map/all_gather | solution.py:14
  816.2 23.9 %all-gather.31.cloned.1.call-done = f32[4096,512]{1,0:T(8,128)} async-done(((f32[512,512]{1,0:T(8,128)}), f32[4096,512]{1,0:T(8,128)}) %all-gather.31.cloned.1.call-update) | async-done | bytes 8388624 | tf_op jit(solution)/shard_map/all_gather | solution.py:14
  840.1 4.5 reduce_sum.96
  848.4 11.7 %cholesky.358 = f32[128,128]{1,0:T(8,128)S(1)} custom-call(f32[128,128]{1,0:T(8,128)S(1)} %cholesky.439), custom_call_target="Cholesky" | custom-call | tf_op jit(solution)/shard_map/jit(cholesky)/cholesky | solution.py:84
  860.3 9.8 custom-call.40
  872.6 11.8 %cholesky.377 = f32[128,128]{1,0:T(8,128)S(1)} custom-call(f32[128,128]{1,0:T(8,128)S(1)} %cholesky.443), custom_call_target="Cholesky" | custom-call | tf_op jit(solution)/shard_map/jit(cholesky)/cholesky | solution.py:84
  884.5 9.8 custom-call.41
  895.9 11.7 %cholesky.398 = f32[128,128]{1,0:T(8,128)S(1)} custom-call(f32[128,128]{1,0:T(8,128)S(1)} %cholesky.448), custom_call_target="Cholesky" | custom-call | tf_op jit(solution)/shard_map/jit(cholesky)/cholesky | solution.py:84
  907.6 9.8 custom-call.42
  918.9 11.9 %cholesky.415 = f32[128,128]{1,0:T(8,128)S(1)} custom-call(f32[128,128]{1,0:T(8,128)S(1)} %convolution_subtract_fusion.16), custom_call_target="Cholesky" | custom-call | tf_op jit(solution)/shard_map/jit(cholesky)/cholesky | solution.py:84
  937.0 11.7 %while.15 = (s32[]{:T(128)}, f32[512,512]{1,0:T(8,128)}, s32[4,2]{0,1:T(2,128)S(1)}, f32[4,128,128]{2,1,0:T(8,128)S(1)}, s32[]{:T(128)}) while((s32[]{:T(128)}, f32[512,512]{1,0:T(8,128)}, s32[4,2]{0,1:T(2,128)S(1)}, f32[4,128,128]{2,1,0:T(8,128)S(1)}, s32[]{:T(128)}) %tuple.108), condition=%wide.while_cond.2.clone, body=%wide.while_body.2.clone.sunk | while | flops 2 | bytes 131181 | solution.py:85
  937.7 2.2 bitcast_dynamic-update-slice_fusion.5
  940.6 2.2 bitcast_dynamic-update-slice_fusion.5
  948.7 39.3 %custom-call.43 = f32[4,128,128]{1,2,0:T(8,128)S(1)} custom-call(f32[4,128,128]{2,1,0:T(8,128)S(1)} %get-tuple-element.74), custom_call_target="InvertDiagBlocksLowerTriangular" | custom-call | tf_op jit(solution)/shard_map/triangular_solve/custom-call.3 | solution.py:85
  996.9 9.4 reduce_sum.97
  1013.3 3.0 fusion.29
  1018.2 4.9 convolution_subtract_fusion
  (208 shorter events, 89.9 us)
Async XLA Ops:
  7.2 1.6 copy-start
  7.2 186.9 %all-gather.21.cloned.1.call-start = ((), (), s32[]{:S(2)}) async-start(), calls=%async_computation.2 | async-start | bytes 10485760 | tf_op jit(solution)/shard_map/all_gather | solution.py:61
  8.7 3.5 copy-start.27
  8.7 3.6 copy-start.28
  8.7 3.6 copy-start.29
  19.5 7.6 copy-start.4
  27.1 1.3 copy-start.5
  46.1 320.6 %all-gather.19.cloned.1.call-start = ((), (), s32[]{:S(2)}) async-start(), calls=%async_computation.1 | async-start | bytes 18874368 | tf_op jit(solution)/shard_map/all_gather | solution.py:60
  202.0 131.9 %all-to-all-start = ((bf16[8,512,1024]{1,2,0:T(8,128)(2,1)}), bf16[8,512,1024]{1,2,0:T(8,128)(2,1)}, u32[]{:S(2)}, u32[]{:S(2)}) async-start(bf16[8,512,1024]{1,2,0:T(8,128)(2,1)} %bitcast.266), calls=%async_computation | async-start | bytes 16777216 | tf_op jit(solution)/shard_map/all_to_all | solution.py:62
  207.0 258.5 %all-gather.23.cloned.1.call-start = ((), (), s32[]{:S(2)}) async-start(), calls=%async_computation.3 | async-start | bytes 5242880 | tf_op jit(solution)/shard_map/all_gather | solution.py:14
  382.6 1.4 copy-start.10
  385.1 137.2 %all-gather.25.cloned.1.call-start = ((), (), s32[]{:S(2)}) async-start(), calls=%async_computation.4 | async-start | bytes 9437184 | tf_op jit(solution)/shard_map/all_gather | solution.py:14
  469.4 204.8 %all-gather.27.cloned.1.call-start = ((), (), s32[]{:S(2)}) async-start(), calls=%async_computation.5 | async-start | bytes 18874368 | tf_op jit(solution)/shard_map/all_gather | solution.py:14
  469.9 313.4 %all-gather.29.cloned.1.call-start = ((), (), s32[]{:S(2)}) async-start(), calls=%async_computation.6 | async-start | bytes 5242880 | tf_op jit(solution)/shard_map/all_gather | solution.py:14
  529.5 1.0 copy-start.15
  630.1 41.4 %copy-start.8 = (f32[512,512]{1,0:T(8,128)S(1)}, f32[512,512]{1,0:T(8,128)}, u32[]{:S(2)}) copy-start(f32[512,512]{1,0:T(8,128)} %get-tuple-element.246) | copy-start | bytes 3145732
  669.4 14.2 %copy-start.17 = (f32[4,128,128]{1,2,0:T(8,128)}, f32[4,128,128]{1,2,0:T(8,128)S(1)}, u32[]{:S(2)}) copy-start(f32[4,128,128]{1,2,0:T(8,128)S(1)} %custom-call.38) | copy-start | bytes 786436
  671.5 2.7 copy-start.13
  672.4 1.8 copy-start.20
  683.6 5.4 copy-start.7
  685.5 5.4 copy-start.18
  691.5 8.4 copy-start.12
  691.5 3.6 copy-start.11
  691.5 3.6 copy-start.14
  691.5 3.6 copy-start.21
  691.5 3.6 copy-start.24
  695.1 4.8 copy-start.22
  699.9 1.4 copy-start.2
  702.4 137.7 %all-gather.31.cloned.1.call-start = ((), (), s32[]{:S(2)}) async-start(), calls=%async_computation.7 | async-start | bytes 9437184 | tf_op jit(solution)/shard_map/all_gather | solution.py:14
  787.2 0.8 copy-start.25
  787.2 12.8 %copy-start.19 = (f32[4,128,128]{1,2,0:T(8,128)S(1)}, f32[4,128,128]{1,2,0:T(8,128)}, u32[]{:S(2)}) copy-start(f32[4,128,128]{1,2,0:T(8,128)} %copy-done.17) | copy-start | bytes 786436
  787.2 209.7 %all-gather.33.cloned.1.call-start = ((), (), s32[]{:S(2)}) async-start(), calls=%async_computation.8 | async-start | bytes 18874368 | tf_op jit(solution)/shard_map/all_gather | solution.py:14
  847.4 1.0 copy-start.16
  948.7 45.6 %copy-start.9 = (f32[512,512]{1,0:T(8,128)S(1)}, f32[512,512]{1,0:T(8,128)}, u32[]{:S(2)}) copy-start(f32[512,512]{1,0:T(8,128)} %get-tuple-element.247) | copy-start | bytes 3145732
  1006.3 4.5 copy-start.6
  1016.3 1.8 copy-start.3
  1016.3 1.8 copy-start.23
  1018.1 5.5 copy-start.1
  1023.0 0.6 copy-start.26
Sparse Core Ops, SparseCore 0:
  46.2 147.8 all-gather.20
  196.0 170.6 all-gather.18
  385.2 80.2 all-gather.22
  469.5 52.7 all-gather.24
  524.6 89.8 all-gather.26
  702.5 80.7 all-gather.28
  787.3 52.7 all-gather.30
  842.6 89.7 all-gather.32
